TPU v7x, 32 devices: a whole 2x2x4 slice. The times are simulated.
32 devices in a mesh: ens: 2 (over y), wide: 4 (over z), lev: 2 (over x), fld: 2 (over core).
Axes of the slice: x: 2, y: 2, z: 4, core: 2. Of those that a mesh axis runs over, the one named last changes fastest.
Arguments:
- fourier_input_rows: bfloat16 [4, 1280, 4, 4, 256], P('ens', 'wide', None, 'fld', 'lev'), parts along dimension 0, may hold values from -6 to 6
- legendre: bfloat16 [4, 1280, 1280], P('wide', ('lev', 'fld')), may hold values from -0.15625 to 0.15625
- slot_wave: int32 [4], P('wide'), may hold values from 0 to 1279, as said below
- to_modes: bfloat16 [128, 128], replicated, may hold values from -0.5 to 0.5
- from_modes: bfloat16 [128, 128], replicated, may hold values from -0.5 to 0.5
- mode_rate: float32 [128], replicated, may hold values from 0.05 to 5
Outputs:
- fourier_out: bfloat16 [4, 1280, 4, 4, 256], P('ens', 'wide', None, 'fld', 'lev'), parts along dimension 0
- spectral: bfloat16 [8, 1280, 4, 256], P(('ens', 'wide'), None, 'fld', 'lev'), parts along dimension 0
There are 2 independent parts, one for each index of `ens`. A program takes and returns all parts, laid end to end along the dimension named above; an argument that names none is the same for every part. Nothing has to cross between parts.
Inputs may be any that keep to these rules, and one draw needn't show every extreme that they name: `slot_wave`: the wavenumbers of the slots are distinct; one slot holds 0 and one holds 1279.
All inputs are finite; a program needn't handle non-finite values.
Results may differ from a plain program's by a relative error of at most 0.0065.
Values may be sent and summed in bfloat16 or wider, within the bound.
A program may use at most 64 MiB of HBM per device.

v0:
```python
import math

import jax
import jax.numpy as jnp
from jax import lax
from jax.sharding import PartitionSpec as P


def latitude_weights(count):
    position = jnp.arange(count, dtype=jnp.float32)
    return jnp.sin(math.pi * (position + 0.5) / (2 * count))


def project(level_grid, degree_real, weight_rows, rate_rows, degree_total):
    projected = jnp.einsum(
        "kl,snflr->snfkr", weight_rows, level_grid, preferred_element_type=jnp.float32
    )
    factor = 1.0 + degree_real[:, None] * (degree_real[:, None] + 1.0) * rate_rows[None, :] / (
        degree_total * degree_total
    )
    return (projected / factor[None, :, None, :, None]).astype(jnp.bfloat16)


def shards(fourier_input_rows, legendre, slot_wave, to_modes, from_modes, mode_rate):
    wave_rows = lax.all_to_all(fourier_input_rows, "wide", split_axis=2, concat_axis=1, tiled=True)
    half_count = wave_rows.shape[1]
    slot_count = wave_rows.shape[2]
    field_count = wave_rows.shape[3]
    column_count = wave_rows.shape[4]
    degree_count = legendre.shape[1] * lax.axis_size(("lev", "fld"))
    weights = latitude_weights(half_count)[:, None, None, None]
    north_half = wave_rows[0].astype(jnp.float32)
    south_half = wave_rows[1].astype(jnp.float32)
    symmetric = (weights * (north_half + south_half)).astype(jnp.bfloat16)
    antisym = (weights * (north_half - south_half)).astype(jnp.bfloat16)
    paired = jnp.concatenate((symmetric, antisym), axis=3)

    def direct_rows(section, first_row):
        row_count = section.shape[1]
        degree = first_row + jnp.arange(row_count, dtype=jnp.int32)
        relative = degree[None, :] - slot_wave[:, None]
        product = jnp.einsum("snj,jsfc->snfc", section, paired, preferred_element_type=jnp.float32)
        is_even = (relative % 2 == 0)[:, :, None, None]
        is_live = (relative >= 0)[:, :, None, None]
        picked = jnp.where(is_even, product[..., :column_count], product[..., column_count:])
        return jnp.where(is_live, picked, jnp.zeros_like(picked))

    full_table = lax.all_gather(legendre, ("lev", "fld"), axis=1, tiled=True)
    block_rows = 128
    block_count = degree_count // block_rows

    def direct_step(block_index, buffer):
        first_row = block_index * block_rows
        section = lax.dynamic_slice_in_dim(full_table, first_row, block_rows, 1)
        result = direct_rows(section, first_row).astype(jnp.bfloat16)
        return lax.dynamic_update_slice_in_dim(buffer, result, first_row, 1)

    initial_raw = jnp.zeros((slot_count, degree_count, field_count, column_count), jnp.bfloat16)
    raw_spectral = lax.fori_loop(0, block_count, direct_step, initial_raw)
    own_levels = column_count // 2
    first_level = lax.axis_index("lev") * own_levels
    degree_real = jnp.arange(degree_count, dtype=jnp.float32)
    all_levels = lax.all_gather(raw_spectral, "lev", axis=3, tiled=True)
    level_count = all_levels.shape[3] // 2
    level_grid = all_levels.reshape(slot_count, degree_count, field_count, level_count, 2)
    weight_rows = lax.dynamic_slice_in_dim(to_modes, first_level, own_levels, 0)
    rate_rows = lax.dynamic_slice_in_dim(mode_rate, first_level, own_levels, 0)
    own_modes = project(level_grid, degree_real, weight_rows, rate_rows, degree_count).reshape(
        slot_count, degree_count, field_count, column_count
    )
    mode_values = lax.all_gather(own_modes, "lev", axis=3, tiled=True).reshape(
        slot_count, degree_count, field_count, level_count, 2
    )
    back_rows = lax.dynamic_slice_in_dim(from_modes, first_level, own_levels, 0)
    spectral = jnp.einsum(
        "lk,snfkr->snflr", back_rows, mode_values, preferred_element_type=jnp.float32
    )
    spectral = spectral.astype(jnp.bfloat16).reshape(
        slot_count, degree_count, field_count, column_count
    )

    def inverse_rows(running, section, first_row):
        row_count = section.shape[1]
        degree = first_row + jnp.arange(row_count, dtype=jnp.int32)
        relative = degree[None, :] - slot_wave[:, None]
        spec_rows = lax.dynamic_slice_in_dim(spectral, first_row, row_count, 1)
        even_mask = ((relative >= 0) & (relative % 2 == 0))[:, :, None, None]
        odd_mask = ((relative >= 0) & (relative % 2 == 1))[:, :, None, None]
        empty_rows = jnp.zeros_like(spec_rows)
        parity_split = jnp.concatenate(
            (
                jnp.where(even_mask, spec_rows, empty_rows),
                jnp.where(odd_mask, spec_rows, empty_rows),
            ),
            axis=3,
        )
        return running + jnp.einsum(
            "snj,snfc->jsfc", section, parity_split, preferred_element_type=jnp.float32
        )

    initial_sum = jnp.zeros((half_count, slot_count, field_count, 2 * column_count), jnp.float32)

    def inverse_step(block_index, running):
        first_row = block_index * block_rows
        section = lax.dynamic_slice_in_dim(full_table, first_row, block_rows, 1)
        return inverse_rows(running, section, first_row)

    running = lax.fori_loop(0, block_count, inverse_step, initial_sum)
    even_sum = running[..., :column_count]
    odd_sum = running[..., column_count:]
    fourier_wave = jnp.stack((even_sum + odd_sum, even_sum - odd_sum), axis=0).astype(jnp.bfloat16)
    fourier_out = lax.all_to_all(fourier_wave, "wide", split_axis=1, concat_axis=2, tiled=True)
    return (fourier_out, spectral)


def solution(mesh):
    in_specs = (
        P("ens", "wide", None, "fld", "lev"),
        P("wide", ("lev", "fld"), None),
        P("wide"),
        P(),
        P(),
        P(),
    )
    out_specs = (P("ens", "wide", None, "fld", "lev"), P(("ens", "wide"), None, "fld", "lev"))
    return jax.shard_map(shards, mesh=mesh, in_specs=in_specs, out_specs=out_specs, check_vma=False)
```

profile of v0, /device:TPU:0, one launch (start us, length us, event | category | flops | bytes accessed | tf_op | source)
XLA Modules:
  0.0 206.5 jit_solution(15960541568794821746)
XLA Ops:
  7.2 0.7 all-gather.4.cloned.1.call-update
  7.9 3.3 %copy.24 = bf16[2,320,4,2,128]{4,3,1,0,2:T(2,128)(2,1)} copy(bf16[2,320,4,2,128]{4,3,2,1,0:T(2,128)(2,1)} %param.10) | data formatting | bytes 2621440 | tf_op args[0]
  11.2 6.3 %all-to-all-start = ((bf16[2,320,4,2,128]{4,3,1,0,2:T(2,128)(2,1)}), bf16[2,320,4,2,128]{4,3,1,0,2:T(2,128)(2,1)S(1)}, u32[]{:S(2)}, u32[]{:S(2)}) async-start(bf16[2,320,4,2,128]{4,3,1,0,2:T(2,128)(2,1)} %copy.24), calls=%async_computation | async-start | bytes 2621440 | tf_op jit(solution)/shard_map/all_to_all | solution.py:25
  17.6 31.3 %all-to-all-done = bf16[2,320,4,2,128]{4,3,1,0,2:T(2,128)(2,1)S(1)} async-done(((bf16[2,320,4,2,128]{4,3,1,0,2:T(2,128)(2,1)}), bf16[2,320,4,2,128]{4,3,1,0,2:T(2,128)(2,1)S(1)}, u32[]{:S(2)}, u32[]{:S(2)}) %all-to-all-start) | async-done | bytes 1310752 | tf_op jit(solution)/shard_map/all_to_all | solution.py:25
  48.8 0.9 convert_add_fusion
  49.8 0.3 fusion.29
  50.3 21.4 %while.31 = (s32[]{:T(128)}, bf16[1,1280,2,128]{3,1,2,0:T(8,128)(2,1)S(1)}, s32[1]{0:T(128)}, bf16[1,1280,1280]{2,1,0:T(8,128)(2,1)}, bf16[1280,1,2,256]{3,0,2,1...) while((s32[]{:T(128)}, bf16[1,1280,2,128]{3,1,2,0:T(8,128)(2,1)S(1)}, s32[1]{0:T(128)}, ...), condition=%wide.region_1.2_spmd, body=%wide.region_0.1_spmd.sunk | while | flops 167839616 | bytes 1967515 | solution.py:59
  50.4 1.3 fusion.47
  51.7 0.7 fusion.48
  52.5 1.3 fusion.47
  53.8 0.7 fusion.48
  54.6 1.3 fusion.47
  56.0 0.7 fusion.48
  56.8 1.3 fusion.47
  58.1 0.7 fusion.48
  58.9 1.3 fusion.47
  60.2 0.7 fusion.48
  61.1 1.3 fusion.47
  62.4 0.7 fusion.48
  63.2 1.3 fusion.47
  64.5 0.7 fusion.48
  65.3 1.3 fusion.47
  66.7 0.7 fusion.48
  67.5 1.3 fusion.47
  68.8 0.7 fusion.48
  69.6 1.3 fusion.47
  70.9 0.7 fusion.48
  71.8 0.8 copy-done.1
  72.9 23.2 %all-gather.6.cloned.1.call-done = bf16[1,1280,2,256]{3,1,2,0:T(8,128)(2,1)} async-done(((bf16[1,1280,2,128]{3,1,2,0:T(8,128)(2,1)}), bf16[1,1280,2,256]{3,1,2,0:T(8,128)(2,1)}) %all-gather.6.cloned.1.call-update) | async-done | bytes 1310736 | tf_op jit(solution)/shard_map/all_gather | solution.py:63
  96.1 3.6 %copy.27 = bf16[1,1280,2,256]{1,2,3,0:T(2,128)(2,1)S(1)} copy(bf16[1,1280,2,256]{3,1,2,0:T(8,128)(2,1)} %all-gather.6.cloned.1.call-done) | data formatting | bytes 2621440 | tf_op jit(solution)/shard_map/all_gather | solution.py:63
  99.7 0.3 fusion.25
  100.1 1.5 copy.29
  101.6 24.4 %all-gather.8.cloned.1.call-done = bf16[1,1280,2,256]{1,2,0,3:T(2,128)(2,1)} async-done(((bf16[1,1280,2,128]{1,2,0,3:T(2,128)(2,1)}), bf16[1,1280,2,256]{1,2,0,3:T(2,128)(2,1)}) %all-gather.8.cloned.1.call-update) | async-done | bytes 1310736 | tf_op jit(solution)/shard_map/all_gather | solution.py:71
  126.0 1.6 fusion.22
  127.7 0.7 copy.32
  128.4 25.0 %while.32 = (s32[]{:T(128)}, f32[1280,1,2,256]{0,3,2,1:T(8,128)S(1)}, s32[1]{0:T(128)}, bf16[1,1280,2,128]{1,2,3,0:T(2,128)(2,1)S(1)}, bf16[1,1280,1280]{2,1,0:T...) while((s32[]{:T(128)}, f32[1280,1,2,256]{0,3,2,1:T(8,128)S(1)}, s32[1]{0:T(128)}, ...), condition=%wide.region_3.4_spmd.clone, body=%wide.region_2.3_spmd.clone.sunk | while | flops 169412864 | bytes 6029989 | solution.py:108
  128.4 0.7 compare_and_fusion.3
  129.1 1.7 fusion.51
  130.9 0.7 compare_and_fusion.3
  131.6 1.7 fusion.51
  133.4 0.7 compare_and_fusion.3
  134.1 1.7 fusion.51
  135.9 0.7 compare_and_fusion.3
  136.6 1.7 fusion.51
  138.4 0.7 compare_and_fusion.3
  139.1 1.7 fusion.51
  140.9 0.7 compare_and_fusion.3
  141.6 1.7 fusion.51
  143.4 0.7 compare_and_fusion.3
  144.1 1.7 fusion.51
  145.9 0.7 compare_and_fusion.3
  146.6 1.7 fusion.51
  148.4 0.7 compare_and_fusion.3
  149.1 1.7 fusion.51
  151.0 0.7 compare_and_fusion.3
  151.6 1.7 fusion.51
  153.4 3.1 %copy.34 = f32[1280,1,2,256]{3,2,0,1:T(2,128)} copy(f32[1280,1,2,256]{0,3,2,1:T(8,128)S(1)} %get-tuple-element.269) | data formatting | bytes 5242880 | tf_op jit(solution)/shard_map/while | solution.py:108
  156.5 2.2 %fusion.30 = (bf16[1,1280,1,2,128]{4,3,0,2,1:T(2,128)(2,1)S(1)}, bf16[1,1280,1,2,128]{4,3,0,2,1:T(2,128)(2,1)S(1)}) fusion(f32[1280,1,2,256]{3,2,0,1:T(2,128)} %copy.34), kind=kLoop, calls=%fused_computation.54 | loop fusion | flops 1310720 | bytes 3932160 | tf_op jit(solution)/shard_map/stack | solution.py:111
  158.7 2.7 %pad_maximum_fusion.1 = bf16[2,1280,1,2,128]{4,3,0,2,1:T(2,128)(2,1)} fusion(bf16[1,1280,1,2,128]{4,3,0,2,1:T(2,128)(2,1)S(1)} %get-tuple-element.334, bf16[1,1280,1,2,128]{4,3,0,2,1:T(2,128)(2,1)S(1)} %get-tuple-element.333), kind=kLoop, calls=%fused_computation.45 | loop fusion | flops 655360 | bytes 2621440 | tf_op jit(solution)/shard_map/stack | solution.py:111
  161.5 4.6 %all-to-all-start.1 = ((bf16[2,1280,1,2,128]{4,3,0,2,1:T(2,128)(2,1)}), bf16[2,1280,1,2,128]{4,3,0,2,1:T(2,128)(2,1)S(1)}, u32[]{:S(2)}, u32[]{:S(2)}) async-start(bf16[2,1280,1,2,128]{4,3,0,2,1:T(2,128)(2,1)} %pad_maximum_fusion.1), calls=%async_computation.1 | async-start | bytes 2621440 | tf_op jit(solution)/shard_map/all_to_all | solution.py:112
  166.1 2.1 %copy.39 = bf16[1,1280,2,128]{3,2,1,0:T(2,128)(2,1)} copy(bf16[1,1280,2,128]{1,2,3,0:T(2,128)(2,1)S(1)} %get-tuple-element.472) | data formatting | bytes 1310720
  168.2 29.2 %all-to-all-done.1 = bf16[2,1280,1,2,128]{4,3,0,2,1:T(2,128)(2,1)S(1)} async-done(((bf16[2,1280,1,2,128]{4,3,0,2,1:T(2,128)(2,1)}), bf16[2,1280,1,2,128]{4,3,0,2,1:T(2,128)(2,1)S(1)}, u32[]{:S(2)}, u32[]{:S(2)}) %all-to-all-start.1) | async-done | bytes 1310752 | tf_op jit(solution)/shard_map/all_to_all | solution.py:112
  197.4 0.2 copy.37
  197.6 2.4 %copy.38 = bf16[2,320,4,2,128]{4,3,2,1,0:T(2,128)(2,1)} copy(bf16[2,320,4,2,128]{4,1,2,3,0:T(8,128)(2,1)S(1)} %bitcast.88) | data formatting | bytes 2621440
  (50 shorter events, 2.5 us)
Async XLA Ops:
  7.2 92.5 %copy-start = (bf16[128,128]{1,0:T(8,128)(2,1)S(1)}, bf16[128,128]{1,0:T(8,128)(2,1)}, u32[]{:S(2)}) copy-start(bf16[128,128]{1,0:T(8,128)(2,1)} %param.13) | copy-start | bytes 98308
  7.2 43.1 %all-gather.4.cloned.1.call-start = ((), (), s32[]{:S(2)}) async-start(), calls=%async_computation.2 | async-start | bytes 4096000 | tf_op jit(solution)/shard_map/all_gather | solution.py:48
  11.2 37.7 %all-to-all-start = ((bf16[2,320,4,2,128]{4,3,1,0,2:T(2,128)(2,1)}), bf16[2,320,4,2,128]{4,3,1,0,2:T(2,128)(2,1)S(1)}, u32[]{:S(2)}, u32[]{:S(2)}) async-start(bf16[2,320,4,2,128]{4,3,1,0,2:T(2,128)(2,1)} %copy.24), calls=%async_computation | async-start | bytes 2621440 | tf_op jit(solution)/shard_map/all_to_all | solution.py:25
  17.5 78.6 %all-gather.6.cloned.1.call-start = ((), (), s32[]{:S(2)}) async-start(), calls=%async_computation.3 | async-start | bytes 1966080 | tf_op jit(solution)/shard_map/all_gather | solution.py:63
  50.3 22.3 %copy-start.3 = (f32[128]{0:T(128)S(1)}, f32[128]{0:T(128)}, u32[]{:S(2)}) copy-start(f32[128]{0:T(128)} %param.15) | copy-start | bytes 1540
  71.7 0.8 copy-start.1
  72.6 53.4 %all-gather.8.cloned.1.call-start = ((), (), s32[]{:S(2)}) async-start(), calls=%async_computation.4 | async-start | bytes 1966080 | tf_op jit(solution)/shard_map/all_gather | solution.py:71
  100.1 26.0 %copy-start.2 = (bf16[128,128]{1,0:T(8,128)(2,1)S(1)}, bf16[128,128]{1,0:T(8,128)(2,1)}, u32[]{:S(2)}) copy-start(bf16[128,128]{1,0:T(8,128)(2,1)} %param.14) | copy-start | bytes 98308
  161.5 35.9 %all-to-all-start.1 = ((bf16[2,1280,1,2,128]{4,3,0,2,1:T(2,128)(2,1)}), bf16[2,1280,1,2,128]{4,3,0,2,1:T(2,128)(2,1)S(1)}, u32[]{:S(2)}, u32[]{:S(2)}) async-start(bf16[2,1280,1,2,128]{4,3,0,2,1:T(2,128)(2,1)} %pad_maximum_fusion.1), calls=%async_computation.1 | async-start | bytes 2621440 | tf_op jit(solution)/shard_map/all_to_all | solution.py:112
Sparse Core Ops, SparseCore 0:
  9.6 31.9 all-gather.3
  72.7 23.3 all-gather.5
  101.7 24.2 all-gather.7
where the time goes:
time: 208 us; the launch traced here: 207 us
  waiting for transfers between devices  109 us (52%)
  matrix products  32.3 us (16%)
  other arithmetic  21.1 us (10%)
  local copies, waits for them, and re-layouts  18.4 us (9%)
  between operations  13.9 us (7%)
  starting transfers between devices  11 us (5%)
    all_to_all x1, waiting for transfers between devices, shards(): lax.all_to_all(fourier_input_rows, 'wide', split_axis=2, concat_axis=1, t...  31.3 us
    all_to_all x1, waiting for transfers between devices, shards(): lax.all_to_all(fourier_wave, 'wide', split_axis=1, concat_axis=2, tiled=T...  29.2 us
    all_gather x1, waiting for transfers between devices, shards(): lax.all_gather(own_modes, 'lev', axis=3, tiled=True)  24.4 us
    all_gather x1, waiting for transfers between devices, shards(): all_levels = lax.all_gather(raw_spectral, 'lev', axis=3, tiled=True)  23.2 us
    dot_general x10, matrix products, inverse_rows(): jnp.einsum('snj,snfc->jsfc', section, parity_split, preferred_element_typ...  17.2 us
    dot_general x10, matrix products, direct_rows(): jnp.einsum('snj,jsfc->snfc', section, paired, preferred_element_type=jnp....  13.2 us
    unnamed x11, local copies, waits for them, and re-layouts  8.65 us
    and x10, other arithmetic, inverse_rows(): odd_mask = ((relative >= 0) & (relative % 2 == 1))[:, :, None, None]  6.62 us
  transfers between devices with their start and end apart: 5, of which 4 were waited for; matrix products, arithmetic and copies ran while one was open for 3% of the time, Pallas kernels for 0%

commit v1 on v0

v1 whole, which is shorter than its diff:
```python
import functools
import math

import jax
import jax.numpy as jnp
from jax import lax
from jax.experimental import pallas as pl
from jax.experimental.pallas import tpu as pltpu
from jax.sharding import PartitionSpec as P

MESH = pl.DeviceIdType.MESH


def rows_in(total, most):
    size = most
    while total % size:
        size -= 16
    return size


def latitude_weights(first, count, total):
    position = first + jnp.arange(count, dtype=jnp.int32)
    return jnp.sin(math.pi * (position.astype(jnp.float32) + 0.5) / (2 * total))


def expand(matrix_ref, columns):
    levels = matrix_ref.shape[0]
    hot = lax.broadcasted_iota(jnp.int32, (columns, levels), 0) >> 1
    level = lax.broadcasted_iota(jnp.int32, (columns, levels), 1)
    pick = jnp.where(hot == level, 1.0, 0.0).astype(jnp.bfloat16)
    last = (((1,), (1,)), ((), ()))
    tall = lax.dot_general(pick, matrix_ref[...], last, preferred_element_type=jnp.float32)
    wide = lax.dot_general(
        tall.astype(jnp.bfloat16), pick, last, preferred_element_type=jnp.float32
    )
    row = lax.broadcasted_iota(jnp.int32, (columns, columns), 0)
    col = lax.broadcasted_iota(jnp.int32, (columns, columns), 1)
    return jnp.where(((row ^ col) & 1) == 0, wide, 0.0).astype(jnp.bfloat16)


def step(
    sizes, wave_ref, x_ref, leg_ref, to_ref, from_ref, rate_ref,
    out_ref, spec_ref,
    table, turned, waves, raw_out, raw_in, spec_out, parity, sending, into, back,
    in_send, in_recv, leg_send, leg_recv, leg_local, fwd_send, fwd_recv,
    raw_send, raw_recv, spec_send, spec_recv, out_send, out_recv,
):
    wide, lev = sizes
    fields, _, own_rows, pair = x_ref.shape
    columns = pair // 2
    own_degrees, latitudes = leg_ref.shape
    degrees = table.shape[0]
    part = degrees // lev
    me_w = lax.axis_index("wide")
    me_l = lax.axis_index("lev")
    me_f = lax.axis_index("fld")

    barrier = pltpu.get_barrier_semaphore()
    for k in range(1, wide):
        pl.semaphore_signal(
            barrier, 1, device_id={"wide": lax.rem(me_w + k, wide)}, device_id_type=MESH
        )
    for k in range(1, lev):
        pl.semaphore_signal(
            barrier, 1, device_id={"lev": lax.rem(me_l + k, lev)}, device_id_type=MESH
        )
    pl.semaphore_signal(barrier, 1, device_id={"fld": 1 - me_f}, device_id_type=MESH)
    pl.semaphore_wait(barrier, wide + lev - 1)

    def in_copy(f, k):
        there = lax.rem(me_w + k, wide)
        return pltpu.make_async_remote_copy(
            src_ref=x_ref.at[f, there], dst_ref=waves.at[f, me_w],
            send_sem=in_send.at[f, k], recv_sem=in_recv.at[f, k],
            device_id={"wide": there}, device_id_type=MESH,
        )

    def quarter(l, c):
        start = pl.multiple_of((l * 2 + c) * own_degrees, 16)
        return table.at[pl.ds(start, own_degrees)]

    def leg_copy(k):
        there = lax.rem(me_l + k, lev)
        return pltpu.make_async_remote_copy(
            src_ref=leg_ref, dst_ref=quarter(me_l, me_f),
            send_sem=leg_send.at[k], recv_sem=leg_recv.at[k],
            device_id={"lev": there}, device_id_type=MESH,
        )

    def fwd_copy(k):
        owner = lax.rem(me_l - k + lev, lev)
        return pltpu.make_async_remote_copy(
            src_ref=leg_ref if k == 0 else quarter(owner, me_f), dst_ref=quarter(owner, me_f),
            send_sem=fwd_send.at[k], recv_sem=fwd_recv.at[k],
            device_id={"fld": 1 - me_f}, device_id_type=MESH,
        )

    in_copies = [[in_copy(f, k) for k in range(1, wide)] for f in range(fields)]
    leg_copies = [leg_copy(k) for k in range(1, lev)]
    fwd_copies = [fwd_copy(k) for k in range(lev)]
    for copy in in_copies[0]:
        copy.start()
    for copy in leg_copies:
        copy.start()
    fwd_copies[0].start()
    local = [pltpu.make_async_copy(leg_ref, quarter(me_l, me_f), leg_local.at[0])]
    for f in range(fields):
        local.append(
            pltpu.make_async_copy(x_ref.at[f, me_w], waves.at[f, me_w], leg_local.at[1 + f])
        )
    for copy in local:
        copy.start()

    whole_into = expand(to_ref, lev * columns)
    whole_back = expand(from_ref, lev * columns)
    for l in range(lev):
        into[l] = whole_into[l * columns : (l + 1) * columns, :]
        back[l] = whole_back[:, l * columns : (l + 1) * columns]

    for k in range(1, lev):
        leg_copies[k - 1].wait_recv()
        fwd_copies[k].start()
    for copy in in_copies[0]:
        copy.wait_send()
    for f in range(1, fields):
        for copy in in_copies[f]:
            copy.start()
    for copy in local:
        copy.wait()
    for copy in fwd_copies:
        copy.wait_recv()

    @pl.loop(0, degrees // 128)
    def _(i):
        start = pl.multiple_of(i * 128, 128)
        turned[:, pl.ds(start, 128)] = table[pl.ds(start, 128), :].T

    wave = wave_ref[0]
    direct_rows = rows_in(part, 320)
    for f in range(fields):
        for copy in in_copies[f]:
            copy.wait_recv()

        def raw_copy(k):
            there = lax.rem(me_l + k, lev)
            return pltpu.make_async_remote_copy(
                src_ref=raw_out.at[f, k], dst_ref=raw_in.at[f, k],
                send_sem=raw_send.at[f, k], recv_sem=raw_recv.at[f, k],
                device_id={"lev": there}, device_id_type=MESH,
            )

        raw_copies = [raw_copy(k) for k in range(1, lev)]
        for k in [*range(1, lev), 0]:
            there = lax.rem(me_l + k, lev)

            @pl.loop(0, part // direct_rows)
            def _(i):
                first = pl.multiple_of(there * part + i * direct_rows, 16)
                grid = waves[f].reshape(latitudes, pair).astype(jnp.bfloat16)
                product = jnp.dot(
                    table[pl.ds(first, direct_rows), :], grid, preferred_element_type=jnp.float32
                )
                degree = first + lax.broadcasted_iota(jnp.int32, (direct_rows, columns), 0)
                relative = degree - wave
                picked = jnp.where(
                    (relative & 1) == 0, product[:, :columns], product[:, columns:]
                )
                kept = jnp.where(relative >= 0, picked, 0.0)
                here = pl.multiple_of(i * direct_rows, 16)
                raw_out[f, k, pl.ds(here, direct_rows), :] = kept.astype(jnp.bfloat16)

            if k > 0:
                raw_copies[k - 1].start()
        for copy in raw_copies:
            copy.wait_recv()

        def spec_copy(k):
            there = lax.rem(me_l + k, lev)
            return pltpu.make_async_remote_copy(
                src_ref=spec_out.at[f, k],
                dst_ref=spec_ref.at[f, pl.ds(pl.multiple_of(me_l * part, 16), part)],
                send_sem=spec_send.at[f, k], recv_sem=spec_recv.at[f, k],
                device_id={"lev": there}, device_id_type=MESH,
            )

        @pl.loop(0, part // direct_rows)
        def _(i):
            here = pl.multiple_of(i * direct_rows, 16)
            total = jnp.dot(
                raw_out[f, 0, pl.ds(here, direct_rows), :], into[me_l],
                preferred_element_type=jnp.float32,
            )
            for k in range(1, lev):
                total += jnp.dot(
                    raw_in[f, k, pl.ds(here, direct_rows), :], into[lax.rem(me_l - k + lev, lev)],
                    preferred_element_type=jnp.float32,
                )
            first = me_l * part + here
            degree = first + lax.broadcasted_iota(jnp.int32, total.shape, 0)
            degree = degree.astype(jnp.float32)
            factor = 1.0 + degree * (degree + 1.0) * rate_ref[...] / (degrees * degrees)
            modes = (total / factor).astype(jnp.bfloat16)
            for k in range(lev):
                solved = jnp.dot(
                    modes, back[lax.rem(me_l + k, lev)], preferred_element_type=jnp.float32
                ).astype(jnp.bfloat16)
                if k == 0:
                    spec_ref[f, pl.ds(pl.multiple_of(first, 16), direct_rows), :] = solved
                else:
                    spec_out[f, k, pl.ds(here, direct_rows), :] = solved

        spec_copies = [spec_copy(k) for k in range(1, lev)]
        for copy in spec_copies:
            copy.start()
        for copy in spec_copies:
            copy.wait_recv()

        @pl.loop(0, degrees // direct_rows)
        def _(i):
            first = pl.multiple_of(i * direct_rows, 16)
            values = spec_ref[f, pl.ds(first, direct_rows), :]
            degree = first + lax.broadcasted_iota(jnp.int32, (direct_rows, columns), 0)
            relative = degree - wave
            live = jnp.where(relative >= 0, values.astype(jnp.float32), 0.0)
            is_even = (relative & 1) == 0
            parity[pl.ds(first, direct_rows), :columns] = jnp.where(is_even, live, 0.0).astype(
                jnp.bfloat16
            )
            parity[pl.ds(first, direct_rows), columns:] = jnp.where(is_even, 0.0, live).astype(
                jnp.bfloat16
            )

        def out_copy(k):
            there = lax.rem(me_w + k, wide)
            return pltpu.make_async_remote_copy(
                src_ref=sending.at[f, k], dst_ref=out_ref.at[f, me_w],
                send_sem=out_send.at[f, k], recv_sem=out_recv.at[f, k],
                device_id={"wide": there}, device_id_type=MESH,
            )

        out_copies = [out_copy(k) for k in range(1, wide)]
        for k in [*range(1, wide), 0]:
            there = lax.rem(me_w + k, wide)
            first = pl.multiple_of(there * own_rows, 8)
            sums = jnp.dot(
                turned[pl.ds(first, own_rows), :], parity[...], preferred_element_type=jnp.float32
            )
            north = (sums[:, :columns] + sums[:, columns:]).astype(sending.dtype)
            south = (sums[:, :columns] - sums[:, columns:]).astype(sending.dtype)
            if k == 0:
                out_ref[f, me_w, :, :columns] = north
                out_ref[f, me_w, :, columns:] = south
            else:
                sending[f, k, :, :columns] = north
                sending[f, k, :, columns:] = south
                out_copies[k - 1].start()
        if f == 0:
            later = []
        later.append((raw_copies, spec_copies, out_copies))

    for copy in leg_copies + fwd_copies:
        copy.wait_send()
    for f in range(1, fields):
        for copy in in_copies[f]:
            copy.wait_send()
    for raw_copies, spec_copies, out_copies in later:
        for copy in raw_copies + spec_copies:
            copy.wait_send()
        for copy in out_copies:
            copy.wait_send()
            copy.wait_recv()


def shards(fourier_input_rows, legendre, slot_wave, to_modes, from_modes, mode_rate):
    _, own_rows, slots, fields, columns = fourier_input_rows.shape
    wide = lax.axis_size("wide")
    lev = lax.axis_size("lev")
    own_degrees, latitudes = legendre.shape[1:]
    degrees = own_degrees * lev * 2
    part = degrees // lev
    held = jnp.bfloat16 if own_rows % 16 == 0 else jnp.float32
    weights = latitude_weights(lax.axis_index("wide") * own_rows, own_rows, latitudes)
    weights = weights[:, None, None, None]
    north_half = fourier_input_rows[0].astype(jnp.float32)
    south_half = fourier_input_rows[1].astype(jnp.float32)
    symmetric = (weights * (north_half + south_half)).astype(jnp.bfloat16)
    antisym = (weights * (north_half - south_half)).astype(jnp.bfloat16)
    paired = jnp.concatenate((symmetric, antisym), axis=3)
    paired = jnp.transpose(paired, (2, 1, 0, 3)).astype(held)
    rates = jnp.repeat(mode_rate, 2)[None, :]
    vmem = pl.BlockSpec(memory_space=pltpu.VMEM)
    smem = pl.BlockSpec(memory_space=pltpu.SMEM)
    dma = pltpu.SemaphoreType.DMA
    out, spec = pl.pallas_call(
        functools.partial(step, (wide, lev)),
        out_shape=(
            jax.ShapeDtypeStruct((fields, wide, own_rows, 2 * columns), held),
            jax.ShapeDtypeStruct((fields, degrees, columns), jnp.bfloat16),
        ),
        in_specs=[smem, vmem, vmem, vmem, vmem, vmem],
        out_specs=(vmem, vmem),
        scratch_shapes=[
            pltpu.VMEM((degrees, latitudes), jnp.bfloat16),
            pltpu.VMEM((latitudes, degrees), jnp.bfloat16),
            pltpu.VMEM((fields, wide, own_rows, 2 * columns), held),
            pltpu.VMEM((fields, lev, part, columns), jnp.bfloat16),
            pltpu.VMEM((fields, lev, part, columns), jnp.bfloat16),
            pltpu.VMEM((fields, lev, part, columns), jnp.bfloat16),
            pltpu.VMEM((degrees, 2 * columns), jnp.bfloat16),
            pltpu.VMEM((fields, wide, own_rows, 2 * columns), held),
            pltpu.VMEM((lev, columns, lev * columns), jnp.bfloat16),
            pltpu.VMEM((lev, lev * columns, columns), jnp.bfloat16),
            dma((fields, wide)),
            dma((fields, wide)),
            dma((lev,)),
            dma((lev,)),
            dma((1 + fields,)),
            dma((lev,)),
            dma((lev,)),
            dma((fields, lev)),
            dma((fields, lev)),
            dma((fields, lev)),
            dma((fields, lev)),
            dma((fields, wide)),
            dma((fields, wide)),
        ],
        compiler_params=pltpu.CompilerParams(
            collective_id=0, has_side_effects=True, vmem_limit_bytes=56 * 2**20
        ),
    )(slot_wave, paired, legendre[0], to_modes, from_modes, rates)
    halves = out.astype(jnp.bfloat16).reshape(fields, wide, own_rows, 2, columns)
    fourier_out = jnp.transpose(halves, (3, 2, 1, 0, 4))
    spectral = jnp.transpose(spec, (1, 0, 2))[None]
    return (fourier_out, spectral)


def solution(mesh):
    in_specs = (
        P("ens", "wide", None, "fld", "lev"),
        P("wide", ("lev", "fld"), None),
        P("wide"),
        P(),
        P(),
        P(),
    )
    out_specs = (P("ens", "wide", None, "fld", "lev"), P(("ens", "wide"), None, "fld", "lev"))
    return jax.shard_map(shards, mesh=mesh, in_specs=in_specs, out_specs=out_specs, check_vma=False)
```

time: 208 us -> 90.1 us (0.43)
  waiting for transfers between devices: 109 us -> 0 us
  Pallas kernels: 0 us -> 70.6 us
  matrix products: 32.3 us -> 0 us
  other arithmetic: 21.1 us -> 1.72 us
  between operations: 13.9 us -> 1.32 us
  starting transfers between devices: 11 us -> 0 us
  local copies, waits for them, and re-layouts: 18.4 us -> 15.1 us
    pallas_call x0 -> x1, Pallas kernels: none -> 70.6 us  [shards(): pl.pallas_call(functools.partial(step, (wide, lev)), out_shape=(jax.Shape...]
    all_to_all x2 -> x0, waiting for transfers between devices: 60.5 us -> none  [the longest x1 31.3 us: shards(): lax.all_to_all(fourier_input_rows, 'wide', split_axis=2, concat_axis=1, t...]
    all_gather x3 -> x0, waiting for transfers between devices: 47.7 us -> none  [the longest x1 24.4 us: shards(): lax.all_gather(own_modes, 'lev', axis=3, tiled=True)]
    dot_general x22 -> x0, matrix products: 32.3 us -> none  [the longest x10 17.2 us: inverse_rows(): jnp.einsum('snj,snfc->jsfc', section, parity_split, preferred_element_typ...]
    all_to_all x2 -> x0, starting transfers between devices: 10.9 us -> none  [the longest x1 6.32 us: shards(): lax.all_to_all(fourier_input_rows, 'wide', split_axis=2, concat_axis=1, t...]
    and x10 -> x0, other arithmetic: 6.62 us -> none  [inverse_rows(): odd_mask = ((relative >= 0) & (relative % 2 == 1))[:, :, None, None]]
    eq x10 -> x0, other arithmetic: 6.61 us -> none  [direct_rows(): is_even = (relative % 2 == 0)[:, :, None, None]]
    reshape x0 -> x2, local copies, waits for them, and re-layouts: none -> 5.36 us  [shards(): out.astype(jnp.bfloat16).reshape(fields, wide, own_rows, 2, columns)]
  transfers between devices with their start and end apart: 5 -> 0, of which waited for: 4 -> 0; matrix products, arithmetic and copies ran while one was open for 3% -> 0% of each run, Pallas kernels for 0% -> 0%
where the time goes in v1:
time: 90.1 us; the launch traced here: 88.8 us
  Pallas kernels  70.6 us (78%)
  local copies, waits for them, and re-layouts  15.1 us (17%)
  other arithmetic  1.72 us (2%)
  between operations  1.32 us (1%)
    pallas_call x1, Pallas kernels, shards(): pl.pallas_call(functools.partial(step, (wide, lev)), out_shape=(jax.Shape...  70.6 us
    unnamed x3, local copies, waits for them, and re-layouts  6.13 us
    reshape x2, local copies, waits for them, and re-layouts, shards(): out.astype(jnp.bfloat16).reshape(fields, wide, own_rows, 2, columns)  5.36 us
    slice x1, local copies, waits for them, and re-layouts, shards(): north_half = fourier_input_rows[0].astype(jnp.float32)  2.18 us

profile of v1, /device:TPU:0, one launch (start us, length us, event | category | flops | bytes accessed | tf_op | source)
XLA Modules:
  0.0 88.8 jit_solution(18032741618121958459)
XLA Ops:
  1.3 0.7 broadcast_in_dim.7
  2.1 0.7 broadcast_in_dim_reshape.3.rate_ref
  2.8 2.2 %fusion.6 = (bf16[1,320,4,2,128]{4,3,2,1,0:T(2,128)(2,1)S(1)}, bf16[1,320,4,2,128]{4,3,2,1,0:T(2,128)(2,1)S(1)}) fusion(bf16[2,320,4,2,128]{4,3,2,1,0:T(2,128)(2,1)} %param.6), kind=kLoop, calls=%fused_computation.11 | loop fusion | bytes 2621440 | tf_op jit(solution)/shard_map/slice | solution.py:284
  5.0 0.5 fusion.2
  5.4 1.2 %maximum_bitcast_fusion.x_ref = bf16[2,4,320,256]{3,2,1,0:T(8,128)(2,1)} fusion(bf16[320,4,2,128]{3,0,1,2:T(8,128)(2,1)S(1)} %get-tuple-element.11, bf16[320,4,2,128]{3,0,1,2:T(8,128)(2,1)S(1)} %get-tuple-element.10), kind=kLoop, calls=%fused_computation.8 | loop fusion | flops 2621440 | bytes 2621440 | tf_op jit(solution)/shard_map/transpose | solution.py:289
  6.6 70.6 %shard_map.77 = (bf16[2,4,320,256]{3,2,1,0:T(8,128)(2,1)}, bf16[2,1280,128]{2,1,0:T(8,128)(2,1)}) custom-call(s32[1]{0:T(128)S(6)} %copy.24.wave_ref, bf16[2,4,320,256]{3,2,1,0:T(8,128)(2,1)} %maximum_bitcast_fusion.x_ref, bf16[320,1280]{1,0:T(8,128)(2,1)} %bitcast.24, bf16[128,128]{1,0:T(8,128)(2,1)} %to_ref.1, bf16[128,128]{1,0:T(8,128)(2,1)} %from_ref.1, ...), custom_call_target="tpu_custom_call" | custom-call | tf_op jit(solution)/shard_map/pallas_call | solution.py:294
  77.3 3.0 %reshape.19 = bf16[2,4,320,2,128]{4,3,2,1,0:T(2,128)(2,1)S(1)} reshape(bf16[2,4,320,256]{3,2,1,0:T(8,128)(2,1)} %get-tuple-element.4) | data formatting | bytes 2621440 | tf_op jit(solution)/shard_map/reshape | solution.py:331
  80.2 0.0 copy-start
  80.2 2.4 %copy.23 = bf16[2,4,320,2,128]{4,0,1,2,3:T(2,128)(2,1)} copy(bf16[2,4,320,2,128]{4,3,2,1,0:T(2,128)(2,1)S(1)} %reshape.19) | data formatting | bytes 2621440 | tf_op jit(solution)/shard_map/reshape | solution.py:331
  82.6 0.0 copy-done
  82.6 6.1 %copy.15 = bf16[1,1280,2,128]{3,2,1,0:T(2,128)(2,1)} copy(bf16[1,1280,2,128]{3,1,2,0:T(8,128)(2,1)S(1)} %bitcast.25) | data formatting | bytes 1310720
  (1 shorter events, 0.0 us)
Async XLA Ops:
  80.2 2.4 %copy-start = (bf16[2,1280,128]{2,1,0:T(8,128)(2,1)S(1)}, bf16[2,1280,128]{2,1,0:T(8,128)(2,1)}, u32[]{:S(2)}) copy-start(bf16[2,1280,128]{2,1,0:T(8,128)(2,1)} %get-tuple-element.5) | copy-start | bytes 1966084

commit v2 on v1

v2 whole, which is shorter than its diff:
```python
import functools
import math

import jax
import jax.numpy as jnp
import numpy as np
from jax import lax
from jax.experimental import pallas as pl
from jax.experimental.pallas import tpu as pltpu
from jax.sharding import PartitionSpec as P

MESH = pl.DeviceIdType.MESH


def rows_in(total, most):
    size = most
    while total % size:
        size -= 16
    return size


def latitude_weights(total, columns):
    position = np.arange(total, dtype=np.float64)
    weights = np.sin(math.pi * (position + 0.5) / (2 * total)).astype(np.float32)
    return jnp.asarray(np.ascontiguousarray(np.broadcast_to(weights[:, None], (total, columns))))


def expand_rates(rate_ref, columns):
    levels = rate_ref.shape[1]
    hot = lax.broadcasted_iota(jnp.int32, (columns, levels), 0) >> 1
    level = lax.broadcasted_iota(jnp.int32, (columns, levels), 1)
    pick = jnp.where(hot == level, 1.0, 0.0)
    return lax.dot_general(
        jnp.broadcast_to(rate_ref[...], (8, levels)), pick, (((1,), (1,)), ((), ())),
        precision=lax.Precision.HIGHEST, preferred_element_type=jnp.float32,
    )


def expand(matrix_ref, columns):
    levels = matrix_ref.shape[0]
    hot = lax.broadcasted_iota(jnp.int32, (columns, levels), 0) >> 1
    level = lax.broadcasted_iota(jnp.int32, (columns, levels), 1)
    pick = jnp.where(hot == level, 1.0, 0.0).astype(jnp.bfloat16)
    last = (((1,), (1,)), ((), ()))
    tall = lax.dot_general(pick, matrix_ref[...], last, preferred_element_type=jnp.float32)
    wide = lax.dot_general(
        tall.astype(jnp.bfloat16), pick, last, preferred_element_type=jnp.float32
    )
    row = lax.broadcasted_iota(jnp.int32, (columns, columns), 0)
    col = lax.broadcasted_iota(jnp.int32, (columns, columns), 1)
    return jnp.where(((row ^ col) & 1) == 0, wide, 0.0).astype(jnp.bfloat16)


def step(
    sizes, wave_ref, given_ref, weight_ref, leg_ref, to_ref, from_ref, rate_ref,
    fourier_ref, spectral_ref,
    weights, single, x_ref, table, turned, waves, raw_out, raw_in, spec_out, spec_ref, parity,
    sending, out_ref, spec_single, into, back, rates,
    in_send, in_recv, leg_send, leg_recv, local_sem, ens_send, ens_recv, own_send, own_recv,
    fwd_send, fwd_recv, raw_send, raw_recv, spec_send, spec_recv, out_send, out_recv,
):
    ens, wide, lev, chunks = sizes
    fields, _, _, own_rows, columns = x_ref.shape
    own_degrees, latitudes = leg_ref.shape
    degrees = table.shape[0]
    part = degrees // lev
    per_row = wide * fields
    me_e = lax.axis_index("ens")
    me_w = lax.axis_index("wide")
    me_l = lax.axis_index("lev")
    me_f = lax.axis_index("fld")

    barrier = pltpu.get_barrier_semaphore()
    for axis, size, me in (("wide", wide, me_w), ("lev", lev, me_l), ("ens", ens, me_e)):
        for k in range(1, size):
            pl.semaphore_signal(
                barrier, 1, device_id={axis: lax.rem(me + k, size)}, device_id_type=MESH
            )
    pl.semaphore_signal(barrier, 1, device_id={"fld": 1 - me_f}, device_id_type=MESH)

    def quarter(l, c):
        start = pl.multiple_of((l * 2 + c) * own_degrees, 16)
        return table.at[pl.ds(start, own_degrees)]

    weight_rows = pl.multiple_of(me_w * own_rows, 8)
    weight_copy = pltpu.make_async_copy(
        weight_ref.at[pl.ds(weight_rows, own_rows)], weights, local_sem.at[0]
    )
    weight_copy.start()
    table_copy = pltpu.make_async_copy(leg_ref, quarter(me_l, me_f), local_sem.at[1])
    table_copy.start()

    total_rows = own_rows * per_row
    piece = total_rows // 5

    for h in range(2):

        @pl.loop(0, 5)
        def _(i):
            rows = pl.ds(pl.multiple_of(i * piece, 16), piece)
            single[h, rows, :] = given_ref[h, rows, :].astype(jnp.float32)

    weight_copy.wait()
    pl.semaphore_wait(barrier, ens + wide + lev - 2)

    def in_copy(f, k):
        there = lax.rem(me_w + k, wide)
        return pltpu.make_async_remote_copy(
            src_ref=x_ref.at[f, there], dst_ref=waves.at[f, me_w],
            send_sem=in_send.at[f, k], recv_sem=in_recv.at[f, k],
            device_id={"wide": there}, device_id_type=MESH,
        )

    share = own_degrees // (ens * chunks)

    def rows_of(l, c, e, i):
        start = (l * 2 + c) * own_degrees + (e * chunks + i) * share
        return table.at[pl.ds(pl.multiple_of(start, 16), share)]

    def leg_copy(k, i):
        start = pl.multiple_of((me_e * chunks + i) * share, 16)
        return pltpu.make_async_remote_copy(
            src_ref=leg_ref.at[pl.ds(start, share)], dst_ref=rows_of(me_l, me_f, me_e, i),
            send_sem=leg_send.at[k, i], recv_sem=leg_recv.at[k, i],
            device_id={"lev": lax.rem(me_l + k, lev)}, device_id_type=MESH,
        )

    def ens_copy(k, q, i):
        rows = rows_of(lax.rem(me_l - k + lev, lev), me_f, me_e, i)
        return pltpu.make_async_remote_copy(
            src_ref=rows, dst_ref=rows,
            send_sem=ens_send.at[k, q, i], recv_sem=ens_recv.at[k, q, i],
            device_id={"ens": lax.rem(me_e + q, ens)}, device_id_type=MESH,
        )

    def fwd_copy(k, q, i):
        rows = rows_of(
            lax.rem(me_l - k + lev, lev), me_f, lax.rem(me_e - q + ens, ens), i
        )
        return pltpu.make_async_remote_copy(
            src_ref=rows, dst_ref=rows,
            send_sem=fwd_send.at[k, q, i], recv_sem=fwd_recv.at[k, q, i],
            device_id={"fld": 1 - me_f}, device_id_type=MESH,
        )

    own_copy = pltpu.make_async_remote_copy(
        src_ref=leg_ref, dst_ref=quarter(me_l, me_f),
        send_sem=own_send.at[0], recv_sem=own_recv.at[0],
        device_id={"fld": 1 - me_f}, device_id_type=MESH,
    )

    def pair_rows(f, s, ref, slot):
        rows = pl.ds(s * fields + f, own_rows, stride=per_row)
        north = single[0, rows, :]
        south = single[1, rows, :]
        plus = (weights[...] * (north + south)).astype(jnp.bfloat16)
        minus = (weights[...] * (north - south)).astype(jnp.bfloat16)
        ref[f, slot, 0] = plus.astype(ref.dtype)
        ref[f, slot, 1] = minus.astype(ref.dtype)

    order = sorted(range(1, wide), key=lambda k: -min(k, wide - k))
    in_copies = [[in_copy(f, k) for k in order] for f in range(fields)]
    leg_copies = [[leg_copy(k, i) for i in range(chunks)] for k in range(1, lev)]
    ens_copies = [
        [[ens_copy(k, q, i) for i in range(chunks)] for q in range(1, ens)] for k in range(1, lev)
    ]
    fwd_copies = [
        [[fwd_copy(k, q, i) for i in range(chunks)] for q in range(ens)] for k in range(1, lev)
    ]
    for row in leg_copies:
        for copy in row:
            copy.start()
    for k, copy in zip(order, in_copies[0]):
        there = lax.rem(me_w + k, wide)
        pair_rows(0, there, x_ref, there)
        copy.start()
    own_copy.start()
    for f in range(fields):
        pair_rows(f, me_w, waves, me_w)
    for f in range(1, fields):
        for k in order:
            there = lax.rem(me_w + k, wide)
            pair_rows(f, there, x_ref, there)

    rates[...] = expand_rates(rate_ref, lev * columns)
    whole_into = expand(to_ref, lev * columns)
    whole_back = expand(from_ref, lev * columns)
    for l in range(lev):
        into[l] = whole_into[l * columns : (l + 1) * columns, :]
        back[l] = whole_back[:, l * columns : (l + 1) * columns]

    for i in range(chunks + 1):
        for k in range(lev - 1):
            if i < chunks:
                leg_copies[k][i].wait_recv()
                for q in range(ens - 1):
                    ens_copies[k][q][i].start()
                fwd_copies[k][0][i].start()
            if i > 0:
                for q in range(ens - 1):
                    ens_copies[k][q][i - 1].wait_recv()
                    fwd_copies[k][q + 1][i - 1].start()
    for copy in in_copies[0]:
        copy.wait_send()
    for f in range(1, fields):
        for copy in in_copies[f]:
            copy.start()
    table_copy.wait()
    own_copy.wait_recv()
    for k in range(lev - 1):
        for q in range(ens):
            for i in range(chunks):
                fwd_copies[k][q][i].wait_recv()

    def turn():
        @pl.loop(0, degrees // 128)
        def _(i):
            start = pl.multiple_of(i * 128, 128)
            turned[:, pl.ds(start, 128)] = table[pl.ds(start, 128), :].T

    wave = wave_ref[0]
    direct_rows = rows_in(part, 320)
    for f in range(fields):
        for copy in in_copies[f]:
            copy.wait_recv()

        def raw_copy(k):
            there = lax.rem(me_l + k, lev)
            return pltpu.make_async_remote_copy(
                src_ref=raw_out.at[f, k], dst_ref=raw_in.at[f, k],
                send_sem=raw_send.at[f, k], recv_sem=raw_recv.at[f, k],
                device_id={"lev": there}, device_id_type=MESH,
            )

        raw_copies = [raw_copy(k) for k in range(1, lev)]
        for k in [*range(1, lev), 0]:
            there = lax.rem(me_l + k, lev)

            @pl.loop(0, part // direct_rows)
            def _(i):
                first = pl.multiple_of(there * part + i * direct_rows, 16)
                grid = jnp.concatenate(
                    [waves[f, :, h].reshape(latitudes, columns) for h in range(2)], axis=1
                ).astype(jnp.bfloat16)
                product = jnp.dot(
                    table[pl.ds(first, direct_rows), :], grid, preferred_element_type=jnp.float32
                )
                degree = first + lax.broadcasted_iota(jnp.int32, (direct_rows, columns), 0)
                relative = degree - wave
                picked = jnp.where(
                    (relative & 1) == 0, product[:, :columns], product[:, columns:]
                )
                kept = jnp.where(relative >= 0, picked, 0.0)
                here = pl.multiple_of(i * direct_rows, 16)
                raw_out[f, k, pl.ds(here, direct_rows), :] = kept.astype(jnp.bfloat16)

            if k > 0:
                raw_copies[k - 1].start()
        if f == 0:
            turn()
        for copy in raw_copies:
            copy.wait_recv()

        def spec_copy(k):
            there = lax.rem(me_l + k, lev)
            return pltpu.make_async_remote_copy(
                src_ref=spec_out.at[f, k],
                dst_ref=spec_ref.at[f, pl.ds(pl.multiple_of(me_l * part, 16), part)],
                send_sem=spec_send.at[f, k], recv_sem=spec_recv.at[f, k],
                device_id={"lev": there}, device_id_type=MESH,
            )

        @pl.loop(0, part // direct_rows)
        def _(i):
            here = pl.multiple_of(i * direct_rows, 16)
            total = jnp.dot(
                raw_out[f, 0, pl.ds(here, direct_rows), :], into[me_l],
                preferred_element_type=jnp.float32,
            )
            for k in range(1, lev):
                total += jnp.dot(
                    raw_in[f, k, pl.ds(here, direct_rows), :], into[lax.rem(me_l - k + lev, lev)],
                    preferred_element_type=jnp.float32,
                )
            first = me_l * part + here
            degree = first + lax.broadcasted_iota(jnp.int32, total.shape, 0)
            degree = degree.astype(jnp.float32)
            factor = 1.0 + degree * (degree + 1.0) * rates[0:1, :] / (degrees * degrees)
            modes = (total / factor).astype(jnp.bfloat16)
            for k in range(lev):
                solved = jnp.dot(
                    modes, back[lax.rem(me_l + k, lev)], preferred_element_type=jnp.float32
                ).astype(jnp.bfloat16)
                if k == 0:
                    spec_ref[f, pl.ds(pl.multiple_of(first, 16), direct_rows), :] = solved
                else:
                    spec_out[f, k, pl.ds(here, direct_rows), :] = solved

        spec_copies = [spec_copy(k) for k in range(1, lev)]
        for copy in spec_copies:
            copy.start()
        for copy in spec_copies:
            copy.wait_recv()

        @pl.loop(0, degrees // direct_rows)
        def _(i):
            first = pl.multiple_of(i * direct_rows, 16)
            values = spec_ref[f, pl.ds(first, direct_rows), :]
            degree = first + lax.broadcasted_iota(jnp.int32, (direct_rows, columns), 0)
            relative = degree - wave
            values = values.astype(jnp.float32)
            spec_single[pl.ds(first * fields + f, direct_rows, stride=fields), :] = values
            live = jnp.where(relative >= 0, values, 0.0)
            is_even = (relative & 1) == 0
            parity[pl.ds(first, direct_rows), :columns] = jnp.where(is_even, live, 0.0).astype(
                jnp.bfloat16
            )
            parity[pl.ds(first, direct_rows), columns:] = jnp.where(is_even, 0.0, live).astype(
                jnp.bfloat16
            )

        def out_copy(k):
            there = lax.rem(me_w + k, wide)
            return pltpu.make_async_remote_copy(
                src_ref=sending.at[f, k], dst_ref=out_ref.at[f, me_w],
                send_sem=out_send.at[f, k], recv_sem=out_recv.at[f, k],
                device_id={"wide": there}, device_id_type=MESH,
            )

        out_copies = [out_copy(k) for k in order]
        for place, k in enumerate([*order, 0]):
            there = lax.rem(me_w + k, wide)
            first = pl.multiple_of(there * own_rows, 8)
            sums = jnp.dot(
                turned[pl.ds(first, own_rows), :], parity[...], preferred_element_type=jnp.float32
            )
            north = (sums[:, :columns] + sums[:, columns:]).astype(sending.dtype)
            south = (sums[:, :columns] - sums[:, columns:]).astype(sending.dtype)
            if k == 0:
                out_ref[f, me_w, 0] = north
                out_ref[f, me_w, 1] = south
            else:
                sending[f, k, 0] = north
                sending[f, k, 1] = south
                out_copies[place].start()
        if f == 0:
            later = []
        later.append((raw_copies, spec_copies, out_copies))

    @pl.loop(0, degrees // direct_rows)
    def _(i):
        count = direct_rows * fields
        rows = pl.ds(pl.multiple_of(i * count, 16), count)
        spectral_ref[rows, :] = spec_single[rows, :].astype(jnp.bfloat16)

    own_copy.wait_send()
    for k in range(lev - 1):
        for i in range(chunks):
            leg_copies[k][i].wait_send()
            for q in range(ens):
                fwd_copies[k][q][i].wait_send()
            for q in range(ens - 1):
                ens_copies[k][q][i].wait_send()
    for f in range(1, fields):
        for copy in in_copies[f]:
            copy.wait_send()
    for raw_copies, spec_copies, _ in later:
        for copy in raw_copies + spec_copies:
            copy.wait_send()

    def place_rows(f, s):
        for h in range(2):
            rows = pl.ds(s * fields + f, own_rows, stride=per_row)
            single[h, rows, :] = out_ref[f, s, h].astype(jnp.float32)

    for f in range(fields):
        place_rows(f, me_w)
    for f in range(fields):
        for k, copy in zip(order, later[f][2]):
            copy.wait_recv()
            place_rows(f, lax.rem(me_w - k + wide, wide))
    for h in range(2):

        @pl.loop(0, 5)
        def _(i):
            rows = pl.ds(pl.multiple_of(i * piece, 16), piece)
            fourier_ref[h, rows, :] = single[h, rows, :].astype(jnp.bfloat16)

    for f in range(fields):
        for copy in later[f][2]:
            copy.wait_send()


def shards(fourier_input_rows, legendre, slot_wave, to_modes, from_modes, mode_rate):
    _, own_rows, slots, fields, columns = fourier_input_rows.shape
    ens = lax.axis_size("ens")
    wide = lax.axis_size("wide")
    lev = lax.axis_size("lev")
    own_degrees, latitudes = legendre.shape[1:]
    degrees = own_degrees * lev * 2
    part = degrees // lev
    chunks = 5
    held = jnp.bfloat16 if own_rows % 16 == 0 else jnp.float32
    rows = own_rows * slots * fields
    given = fourier_input_rows.reshape(2, rows, columns)
    vmem = pl.BlockSpec(memory_space=pltpu.VMEM)
    smem = pl.BlockSpec(memory_space=pltpu.SMEM)
    dma = pltpu.SemaphoreType.DMA
    blocks = (fields, wide, 2, own_rows, columns)
    swaps = (fields, lev, part, columns)
    out, spec = pl.pallas_call(
        functools.partial(step, (ens, wide, lev, chunks)),
        out_shape=(
            jax.ShapeDtypeStruct((2, rows, columns), jnp.bfloat16),
            jax.ShapeDtypeStruct((degrees * fields, columns), jnp.bfloat16),
        ),
        in_specs=[smem, vmem, pl.BlockSpec(memory_space=pl.ANY), vmem, vmem, vmem, vmem],
        out_specs=(vmem, vmem),
        scratch_shapes=[
            pltpu.VMEM((own_rows, columns), jnp.float32),
            pltpu.VMEM((2, rows, columns), jnp.float32),
            pltpu.VMEM(blocks, held),
            pltpu.VMEM((degrees, latitudes), jnp.bfloat16),
            pltpu.VMEM((latitudes, degrees), jnp.bfloat16),
            pltpu.VMEM(blocks, held),
            pltpu.VMEM(swaps, jnp.bfloat16),
            pltpu.VMEM(swaps, jnp.bfloat16),
            pltpu.VMEM(swaps, jnp.bfloat16),
            pltpu.VMEM((fields, degrees, columns), jnp.bfloat16),
            pltpu.VMEM((degrees, 2 * columns), jnp.bfloat16),
            pltpu.VMEM(blocks, held),
            pltpu.VMEM(blocks, held),
            pltpu.VMEM((degrees * fields, columns), jnp.float32),
            pltpu.VMEM((lev, columns, lev * columns), jnp.bfloat16),
            pltpu.VMEM((lev, lev * columns, columns), jnp.bfloat16),
            pltpu.VMEM((8, lev * columns), jnp.float32),
            dma((fields, wide)),
            dma((fields, wide)),
            dma((lev, chunks)),
            dma((lev, chunks)),
            dma((2,)),
            dma((lev, ens, chunks)),
            dma((lev, ens, chunks)),
            dma((1,)),
            dma((1,)),
            dma((lev, ens, chunks)),
            dma((lev, ens, chunks)),
            dma((fields, lev)),
            dma((fields, lev)),
            dma((fields, lev)),
            dma((fields, lev)),
            dma((fields, wide)),
            dma((fields, wide)),
        ],
        compiler_params=pltpu.CompilerParams(
            collective_id=0, has_side_effects=True, vmem_limit_bytes=56 * 2**20
        ),
    )(
        slot_wave, given, latitude_weights(latitudes, columns), legendre[0],
        to_modes, from_modes, mode_rate[None, :],
    )
    fourier_out = out.reshape(2, own_rows, slots, fields, columns)
    spectral = spec.reshape(1, degrees, fields, columns)
    return (fourier_out, spectral)


def solution(mesh):
    in_specs = (
        P("ens", "wide", None, "fld", "lev"),
        P("wide", ("lev", "fld"), None),
        P("wide"),
        P(),
        P(),
        P(),
    )
    out_specs = (P("ens", "wide", None, "fld", "lev"), P(("ens", "wide"), None, "fld", "lev"))
    return jax.shard_map(shards, mesh=mesh, in_specs=in_specs, out_specs=out_specs, check_vma=False)
```

time: 90.1 us -> 73.3 us (0.81)
  local copies, waits for them, and re-layouts: 15.1 us -> 4.18 us
  Pallas kernels: 70.6 us -> 66.7 us
  other arithmetic: 1.72 us -> 0 us
    reshape x2 -> x0, local copies, waits for them, and re-layouts: 5.36 us -> none  [shards(): out.astype(jnp.bfloat16).reshape(fields, wide, own_rows, 2, columns)]
    pallas_call x1, Pallas kernels: 70.6 us -> 66.7 us  [shards(): pl.pallas_call(functools.partial(step, (ens, wide, lev, chunks)), out_sha...]
    slice x1 -> x0, local copies, waits for them, and re-layouts: 2.18 us -> none  [shards(): north_half = fourier_input_rows[0].astype(jnp.float32)]
    unnamed x3 -> x4, local copies, waits for them, and re-layouts: 6.13 us -> 4.18 us
    transpose x1 -> x0, other arithmetic: 1.21 us -> none  [shards(): paired = jnp.transpose(paired, (2, 1, 0, 3)).astype(held)]
where the time goes in v2:
time: 73.3 us; the launch traced here: 72.2 us
  Pallas kernels  66.7 us (91%)
  local copies, waits for them, and re-layouts  4.18 us (6%)
  between operations  1.29 us (2%)
    pallas_call x1, Pallas kernels, shards(): pl.pallas_call(functools.partial(step, (ens, wide, lev, chunks)), out_sha...  66.7 us
    unnamed x4, local copies, waits for them, and re-layouts  4.18 us

profile of v2, /device:TPU:0, one launch (start us, length us, event | category | flops | bytes accessed | tf_op | source)
XLA Modules:
  0.0 72.2 jit_solution(13996222536376085159)
XLA Ops:
  1.3 66.7 %shard_map.86 = (bf16[2,2560,128]{2,1,0:T(8,128)(2,1)}, bf16[2560,128]{1,0:T(8,128)(2,1)}) custom-call(s32[1]{0:T(128)S(6)} %copy.11.wave_ref, bf16[2,2560,128]{2,1,0:T(8,128)(2,1)} %bitcast.5, f32[1280,128]{1,0:T(8,128)} %constant.2.clone.weight_ref, bf16[320,1280]{1,0:T(8,128)(2,1)} %bitcast.7, bf16[128,128]{1,0:T(8,128)(2,1)} %to_ref.1, ...), custom_call_target="tpu_custom_call" | custom-call | tf_op jit(solution)/shard_map/pallas_call | solution.py:411
  68.0 0.0 copy-start
  68.0 3.3 %copy.12 = bf16[2,320,4,2,128]{4,3,2,1,0:T(2,128)(2,1)} copy(bf16[2,320,4,2,128]{4,3,2,1,0:T(2,128)(2,1)} %bitcast.6) | data formatting | bytes 2621440
  71.3 0.0 copy-done
  71.3 0.8 %copy.13 = bf16[1,1280,2,128]{3,2,1,0:T(2,128)(2,1)} copy(bf16[1,1280,2,128]{3,2,1,0:T(2,128)(2,1)S(1)} %bitcast.8) | data formatting | bytes 1310720
Async XLA Ops:
  68.0 3.3 %copy-start = (bf16[2560,128]{1,0:T(8,128)(2,1)S(1)}, bf16[2560,128]{1,0:T(8,128)(2,1)}, u32[]{:S(2)}) copy-start(bf16[2560,128]{1,0:T(8,128)(2,1)} %get-tuple-element.5) | copy-start | bytes 1966084

commit v3 on v2

--- a/solution.py
+++ b/solution.py
@@ -52,16 +52,16 @@
 
 
 def step(
-    sizes, wave_ref, given_ref, weight_ref, leg_ref, to_ref, from_ref, rate_ref,
+    sizes, wave_ref, given_far, weight_ref, leg_far, to_far, from_far, rate_far,
     fourier_ref, spectral_ref,
-    weights, single, x_ref, table, turned, waves, raw_out, raw_in, spec_out, spec_ref, parity,
+    given_ref, to_ref, from_ref, rate_ref, weights, single, x_ref, table, turned, waves, raw_out, raw_in, spec_out, spec_ref, parity,
     sending, out_ref, spec_single, into, back, rates,
     in_send, in_recv, leg_send, leg_recv, local_sem, ens_send, ens_recv, own_send, own_recv,
     fwd_send, fwd_recv, raw_send, raw_recv, spec_send, spec_recv, out_send, out_recv,
 ):
     ens, wide, lev, chunks = sizes
     fields, _, _, own_rows, columns = x_ref.shape
-    own_degrees, latitudes = leg_ref.shape
+    own_degrees, latitudes = leg_far.shape
     degrees = table.shape[0]
     part = degrees // lev
     per_row = wide * fields
@@ -83,17 +83,26 @@
         return table.at[pl.ds(start, own_degrees)]
 
     weight_rows = pl.multiple_of(me_w * own_rows, 8)
+    given_copies = [
+        pltpu.make_async_copy(given_far.at[h], given_ref.at[h], local_sem.at[h]) for h in range(2)
+    ]
+    table_copy = pltpu.make_async_copy(leg_far, quarter(me_l, me_f), local_sem.at[2])
     weight_copy = pltpu.make_async_copy(
-        weight_ref.at[pl.ds(weight_rows, own_rows)], weights, local_sem.at[0]
-    )
-    weight_copy.start()
-    table_copy = pltpu.make_async_copy(leg_ref, quarter(me_l, me_f), local_sem.at[1])
-    table_copy.start()
+        weight_ref.at[pl.ds(weight_rows, own_rows)], weights, local_sem.at[3]
+    )
+    level_copies = [
+        pltpu.make_async_copy(to_far, to_ref, local_sem.at[4]),
+        pltpu.make_async_copy(from_far, from_ref, local_sem.at[5]),
+        pltpu.make_async_copy(rate_far, rate_ref, local_sem.at[6]),
+    ]
+    for copy in [*given_copies, weight_copy, table_copy, *level_copies]:
+        copy.start()
 
     total_rows = own_rows * per_row
     piece = total_rows // 5
 
     for h in range(2):
+        given_copies[h].wait()
 
         @pl.loop(0, 5)
         def _(i):
@@ -118,9 +127,9 @@
         return table.at[pl.ds(pl.multiple_of(start, 16), share)]
 
     def leg_copy(k, i):
-        start = pl.multiple_of((me_e * chunks + i) * share, 16)
+        rows = rows_of(me_l, me_f, me_e, i)
         return pltpu.make_async_remote_copy(
-            src_ref=leg_ref.at[pl.ds(start, share)], dst_ref=rows_of(me_l, me_f, me_e, i),
+            src_ref=rows, dst_ref=rows,
             send_sem=leg_send.at[k, i], recv_sem=leg_recv.at[k, i],
             device_id={"lev": lax.rem(me_l + k, lev)}, device_id_type=MESH,
         )
@@ -144,7 +153,7 @@
         )
 
     own_copy = pltpu.make_async_remote_copy(
-        src_ref=leg_ref, dst_ref=quarter(me_l, me_f),
+        src_ref=quarter(me_l, me_f), dst_ref=quarter(me_l, me_f),
         send_sem=own_send.at[0], recv_sem=own_recv.at[0],
         device_id={"fld": 1 - me_f}, device_id_type=MESH,
     )
@@ -167,6 +176,7 @@
     fwd_copies = [
         [[fwd_copy(k, q, i) for i in range(chunks)] for q in range(ens)] for k in range(1, lev)
     ]
+    table_copy.wait()
     for row in leg_copies:
         for copy in row:
             copy.start()
@@ -182,6 +192,8 @@
             there = lax.rem(me_w + k, wide)
             pair_rows(f, there, x_ref, there)
 
+    for copy in level_copies:
+        copy.wait()
     rates[...] = expand_rates(rate_ref, lev * columns)
     whole_into = expand(to_ref, lev * columns)
     whole_back = expand(from_ref, lev * columns)
@@ -205,7 +217,6 @@
     for f in range(1, fields):
         for copy in in_copies[f]:
             copy.start()
-    table_copy.wait()
     own_copy.wait_recv()
     for k in range(lev - 1):
         for q in range(ens):
@@ -220,59 +231,59 @@
 
     wave = wave_ref[0]
     direct_rows = rows_in(part, 320)
+    pieces = part // direct_rows
     for f in range(fields):
         for copy in in_copies[f]:
             copy.wait_recv()
 
-        def raw_copy(k):
+        def raw_copy(k, i):
             there = lax.rem(me_l + k, lev)
+            rows = pl.ds(i * direct_rows, direct_rows)
             return pltpu.make_async_remote_copy(
-                src_ref=raw_out.at[f, k], dst_ref=raw_in.at[f, k],
-                send_sem=raw_send.at[f, k], recv_sem=raw_recv.at[f, k],
+                src_ref=raw_out.at[f, k, rows], dst_ref=raw_in.at[f, k, rows],
+                send_sem=raw_send.at[f, k, i], recv_sem=raw_recv.at[f, k, i],
                 device_id={"lev": there}, device_id_type=MESH,
             )
 
-        raw_copies = [raw_copy(k) for k in range(1, lev)]
-        for k in [*range(1, lev), 0]:
-            there = lax.rem(me_l + k, lev)
-
-            @pl.loop(0, part // direct_rows)
-            def _(i):
-                first = pl.multiple_of(there * part + i * direct_rows, 16)
-                grid = jnp.concatenate(
-                    [waves[f, :, h].reshape(latitudes, columns) for h in range(2)], axis=1
-                ).astype(jnp.bfloat16)
-                product = jnp.dot(
-                    table[pl.ds(first, direct_rows), :], grid, preferred_element_type=jnp.float32
-                )
-                degree = first + lax.broadcasted_iota(jnp.int32, (direct_rows, columns), 0)
-                relative = degree - wave
-                picked = jnp.where(
-                    (relative & 1) == 0, product[:, :columns], product[:, columns:]
-                )
-                kept = jnp.where(relative >= 0, picked, 0.0)
-                here = pl.multiple_of(i * direct_rows, 16)
-                raw_out[f, k, pl.ds(here, direct_rows), :] = kept.astype(jnp.bfloat16)
-
-            if k > 0:
-                raw_copies[k - 1].start()
+        raw_copies = [[raw_copy(k, i) for i in range(pieces)] for k in range(1, lev)]
+        def direct(k, i):
+            first = pl.multiple_of(lax.rem(me_l + k, lev) * part + i * direct_rows, 16)
+            grid = jnp.concatenate(
+                [waves[f, :, h].reshape(latitudes, columns) for h in range(2)], axis=1
+            ).astype(jnp.bfloat16)
+            product = jnp.dot(
+                table[pl.ds(first, direct_rows), :], grid, preferred_element_type=jnp.float32
+            )
+            degree = first + lax.broadcasted_iota(jnp.int32, (direct_rows, columns), 0)
+            relative = degree - wave
+            picked = jnp.where((relative & 1) == 0, product[:, :columns], product[:, columns:])
+            kept = jnp.where(relative >= 0, picked, 0.0)
+            raw_out[f, k, pl.ds(i * direct_rows, direct_rows), :] = kept.astype(jnp.bfloat16)
+
+        for i in range(pieces):
+            for k in range(1, lev):
+                direct(k, i)
+                raw_copies[k - 1][i].start()
+        for i in range(pieces):
+            direct(0, i)
         if f == 0:
             turn()
-        for copy in raw_copies:
-            copy.wait_recv()
-
-        def spec_copy(k):
+
+        def spec_copy(k, i):
             there = lax.rem(me_l + k, lev)
+            start = pl.multiple_of(me_l * part + i * direct_rows, 16)
             return pltpu.make_async_remote_copy(
-                src_ref=spec_out.at[f, k],
-                dst_ref=spec_ref.at[f, pl.ds(pl.multiple_of(me_l * part, 16), part)],
-                send_sem=spec_send.at[f, k], recv_sem=spec_recv.at[f, k],
+                src_ref=spec_out.at[f, k, pl.ds(i * direct_rows, direct_rows)],
+                dst_ref=spec_ref.at[f, pl.ds(start, direct_rows)],
+                send_sem=spec_send.at[f, k, i], recv_sem=spec_recv.at[f, k, i],
                 device_id={"lev": there}, device_id_type=MESH,
             )
 
-        @pl.loop(0, part // direct_rows)
-        def _(i):
-            here = pl.multiple_of(i * direct_rows, 16)
+        spec_copies = [[spec_copy(k, i) for i in range(pieces)] for k in range(1, lev)]
+        for i in range(pieces):
+            here = i * direct_rows
+            for row in raw_copies:
+                row[i].wait_recv()
             total = jnp.dot(
                 raw_out[f, 0, pl.ds(here, direct_rows), :], into[me_l],
                 preferred_element_type=jnp.float32,
@@ -295,12 +306,10 @@
                     spec_ref[f, pl.ds(pl.multiple_of(first, 16), direct_rows), :] = solved
                 else:
                     spec_out[f, k, pl.ds(here, direct_rows), :] = solved
-
-        spec_copies = [spec_copy(k) for k in range(1, lev)]
-        for copy in spec_copies:
-            copy.start()
-        for copy in spec_copies:
-            copy.wait_recv()
+                    spec_copies[k - 1][i].start()
+        for row in spec_copies:
+            for copy in row:
+                copy.wait_recv()
 
         @pl.loop(0, degrees // direct_rows)
         def _(i):
@@ -365,8 +374,9 @@
         for copy in in_copies[f]:
             copy.wait_send()
     for raw_copies, spec_copies, _ in later:
-        for copy in raw_copies + spec_copies:
-            copy.wait_send()
+        for row in raw_copies + spec_copies:
+            for copy in row:
+                copy.wait_send()
 
     def place_rows(f, s):
         for h in range(2):
@@ -414,9 +424,13 @@
             jax.ShapeDtypeStruct((2, rows, columns), jnp.bfloat16),
             jax.ShapeDtypeStruct((degrees * fields, columns), jnp.bfloat16),
         ),
-        in_specs=[smem, vmem, pl.BlockSpec(memory_space=pl.ANY), vmem, vmem, vmem, vmem],
+        in_specs=[smem] + [pl.BlockSpec(memory_space=pltpu.HBM)] * 6,
         out_specs=(vmem, vmem),
         scratch_shapes=[
+            pltpu.VMEM((2, rows, columns), jnp.bfloat16),
+            pltpu.VMEM(to_modes.shape, jnp.bfloat16),
+            pltpu.VMEM(from_modes.shape, jnp.bfloat16),
+            pltpu.VMEM((1, mode_rate.shape[0]), jnp.float32),
             pltpu.VMEM((own_rows, columns), jnp.float32),
             pltpu.VMEM((2, rows, columns), jnp.float32),
             pltpu.VMEM(blocks, held),
@@ -438,22 +452,22 @@
             dma((fields, wide)),
             dma((lev, chunks)),
             dma((lev, chunks)),
-            dma((2,)),
+            dma((7,)),
             dma((lev, ens, chunks)),
             dma((lev, ens, chunks)),
             dma((1,)),
             dma((1,)),
             dma((lev, ens, chunks)),
             dma((lev, ens, chunks)),
-            dma((fields, lev)),
-            dma((fields, lev)),
-            dma((fields, lev)),
-            dma((fields, lev)),
+            dma((fields, lev, part // rows_in(part, 320))),
+            dma((fields, lev, part // rows_in(part, 320))),
+            dma((fields, lev, part // rows_in(part, 320))),
+            dma((fields, lev, part // rows_in(part, 320))),
             dma((fields, wide)),
             dma((fields, wide)),
         ],
         compiler_params=pltpu.CompilerParams(
-            collective_id=0, has_side_effects=True, vmem_limit_bytes=56 * 2**20
+            collective_id=0, has_side_effects=True, vmem_limit_bytes=36 * 2**20
         ),
     )(
         slot_wave, given, latitude_weights(latitudes, columns), legendre[0],

time: 73.3 us -> 71.9 us (0.981)
  Pallas kernels: 66.7 us -> 61.6 us
  local copies, waits for them, and re-layouts: 4.18 us -> 7.6 us
    pallas_call x1, Pallas kernels: 66.7 us -> 61.6 us  [shards(): pl.pallas_call(functools.partial(step, (ens, wide, lev, chunks)), out_sha...]
    unnamed x4 -> x14, local copies, waits for them, and re-layouts: 4.18 us -> 7.6 us
where the time goes in v3:
time: 71.9 us; the launch traced here: 70.5 us
  Pallas kernels  61.6 us (86%)
  local copies, waits for them, and re-layouts  7.6 us (11%)
  between operations  1.3 us (2%)
    pallas_call x1, Pallas kernels, shards(): pl.pallas_call(functools.partial(step, (ens, wide, lev, chunks)), out_sha...  61.6 us
    unnamed x14, local copies, waits for them, and re-layouts  7.6 us

profile of v3, /device:TPU:0, one launch (start us, length us, event | category | flops | bytes accessed | tf_op | source)
XLA Modules:
  0.0 70.5 jit_solution(15813583455793524394)
XLA Ops:
  1.3 0.0 copy-start
  1.3 1.3 %copy-done = bf16[2,320,4,2,128]{4,3,2,1,0:T(2,128)(2,1)S(1)} copy-done((bf16[2,320,4,2,128]{4,3,2,1,0:T(2,128)(2,1)S(1)}, bf16[2,320,4,2,128]{4,3,2,1,0:T(2,128)(2,1)}, u32[]{:S(2)}) %copy-start) | copy-done | bytes 1310744
  2.6 0.0 copy-start.1
  2.6 1.1 %copy-done.1 = bf16[1,320,1280]{2,1,0:T(8,128)(2,1)S(1)} copy-done((bf16[1,320,1280]{2,1,0:T(8,128)(2,1)S(1)}, bf16[1,320,1280]{2,1,0:T(8,128)(2,1)}, u32[]{:S(2)}) %copy-start.1) | copy-done | bytes 819224
  3.7 0.0 copy-start.2
  3.7 1.1 %copy-done.2 = f32[1280,128]{1,0:T(8,128)S(1)} copy-done((f32[1280,128]{1,0:T(8,128)S(1)}, f32[1280,128]{1,0:T(8,128)}, u32[]{:S(2)}) %copy-start.2) | copy-done | bytes 655384
  4.8 0.0 copy-start.3
  4.8 0.8 %copy-done.3 = bf16[128,128]{1,0:T(8,128)(2,1)S(1)} copy-done((bf16[128,128]{1,0:T(8,128)(2,1)S(1)}, bf16[128,128]{1,0:T(8,128)(2,1)}, u32[]{:S(2)}) %copy-start.3) | copy-done | bytes 32792
  5.6 0.0 copy-start.4
  5.6 0.8 %copy-done.4 = bf16[128,128]{1,0:T(8,128)(2,1)S(1)} copy-done((bf16[128,128]{1,0:T(8,128)(2,1)S(1)}, bf16[128,128]{1,0:T(8,128)(2,1)}, u32[]{:S(2)}) %copy-start.4) | copy-done | bytes 32792
  6.3 0.0 copy-start.5
  6.3 0.7 copy-done.5
  7.0 61.6 %shard_map.86 = (bf16[2,2560,128]{2,1,0:T(8,128)(2,1)S(1)}, bf16[2560,128]{1,0:T(8,128)(2,1)S(1)}) custom-call(s32[1]{0:T(128)S(6)} %copy.11.wave_ref, bf16[2,2560,128]{2,1,0:T(8,128)(2,1)S(1)} %bitcast.5, f32[1280,128]{1,0:T(8,128)S(1)} %copy-done.2, bf16[320,1280]{1,0:T(8,128)(2,1)S(1)} %bitcast.7, bf16[128,128]{1,0:T(8,128)(2,1)S(1)} %copy-done.3, ...), custom_call_target="tpu_custom_call" | custom-call | tf_op jit(solution)/shard_map/pallas_call | solution.py:421
  68.6 1.1 %copy.12 = bf16[2,320,4,2,128]{4,3,2,1,0:T(2,128)(2,1)} copy(bf16[2,320,4,2,128]{4,3,2,1,0:T(2,128)(2,1)S(1)} %bitcast.6) | data formatting | bytes 2621440
  69.7 0.8 %copy.13 = bf16[1,1280,2,128]{3,2,1,0:T(2,128)(2,1)} copy(bf16[1,1280,2,128]{3,2,1,0:T(2,128)(2,1)S(1)} %bitcast.8) | data formatting | bytes 1310720
Async XLA Ops:
  1.3 1.3 %copy-start = (bf16[2,320,4,2,128]{4,3,2,1,0:T(2,128)(2,1)S(1)}, bf16[2,320,4,2,128]{4,3,2,1,0:T(2,128)(2,1)}, u32[]{:S(2)}) copy-start(bf16[2,320,4,2,128]{4,3,2,1,0:T(2,128)(2,1)} %param.7) | copy-start | bytes 3932164
  2.6 1.1 %copy-start.1 = (bf16[1,320,1280]{2,1,0:T(8,128)(2,1)S(1)}, bf16[1,320,1280]{2,1,0:T(8,128)(2,1)}, u32[]{:S(2)}) copy-start(bf16[1,320,1280]{2,1,0:T(8,128)(2,1)} %param.8) | copy-start | bytes 2457604
  3.7 1.1 %copy-start.2 = (f32[1280,128]{1,0:T(8,128)S(1)}, f32[1280,128]{1,0:T(8,128)}, u32[]{:S(2)}) copy-start(f32[1280,128]{1,0:T(8,128)} %constant.2.clone.weight_ref) | copy-start | bytes 1966084
  4.8 0.8 %copy-start.3 = (bf16[128,128]{1,0:T(8,128)(2,1)S(1)}, bf16[128,128]{1,0:T(8,128)(2,1)}, u32[]{:S(2)}) copy-start(bf16[128,128]{1,0:T(8,128)(2,1)} %to_far.1) | copy-start | bytes 98308
  5.6 0.8 %copy-start.4 = (bf16[128,128]{1,0:T(8,128)(2,1)S(1)}, bf16[128,128]{1,0:T(8,128)(2,1)}, u32[]{:S(2)}) copy-start(bf16[128,128]{1,0:T(8,128)(2,1)} %from_far.1) | copy-start | bytes 98308
  6.3 0.7 copy-start.5

commit v4 on v3

--- a/solution.py
+++ b/solution.py
@@ -52,16 +52,16 @@
 
 
 def step(
-    sizes, wave_ref, given_far, weight_ref, leg_far, to_far, from_far, rate_far,
+    sizes, wave_ref, given_ref, weight_ref, leg_ref, to_ref, from_ref, rate_ref,
     fourier_ref, spectral_ref,
-    given_ref, to_ref, from_ref, rate_ref, weights, single, x_ref, table, turned, waves, raw_out, raw_in, spec_out, spec_ref, parity,
+    weights, single, x_ref, table, turned, waves, raw_out, raw_in, spec_out, spec_ref, parity,
     sending, out_ref, spec_single, into, back, rates,
     in_send, in_recv, leg_send, leg_recv, local_sem, ens_send, ens_recv, own_send, own_recv,
     fwd_send, fwd_recv, raw_send, raw_recv, spec_send, spec_recv, out_send, out_recv,
 ):
     ens, wide, lev, chunks = sizes
     fields, _, _, own_rows, columns = x_ref.shape
-    own_degrees, latitudes = leg_far.shape
+    own_degrees, latitudes = leg_ref.shape
     degrees = table.shape[0]
     part = degrees // lev
     per_row = wide * fields
@@ -83,26 +83,17 @@
         return table.at[pl.ds(start, own_degrees)]
 
     weight_rows = pl.multiple_of(me_w * own_rows, 8)
-    given_copies = [
-        pltpu.make_async_copy(given_far.at[h], given_ref.at[h], local_sem.at[h]) for h in range(2)
-    ]
-    table_copy = pltpu.make_async_copy(leg_far, quarter(me_l, me_f), local_sem.at[2])
     weight_copy = pltpu.make_async_copy(
-        weight_ref.at[pl.ds(weight_rows, own_rows)], weights, local_sem.at[3]
-    )
-    level_copies = [
-        pltpu.make_async_copy(to_far, to_ref, local_sem.at[4]),
-        pltpu.make_async_copy(from_far, from_ref, local_sem.at[5]),
-        pltpu.make_async_copy(rate_far, rate_ref, local_sem.at[6]),
-    ]
-    for copy in [*given_copies, weight_copy, table_copy, *level_copies]:
-        copy.start()
+        weight_ref.at[pl.ds(weight_rows, own_rows)], weights, local_sem.at[0]
+    )
+    weight_copy.start()
+    table_copy = pltpu.make_async_copy(leg_ref, quarter(me_l, me_f), local_sem.at[1])
+    table_copy.start()
 
     total_rows = own_rows * per_row
     piece = total_rows // 5
 
     for h in range(2):
-        given_copies[h].wait()
 
         @pl.loop(0, 5)
         def _(i):
@@ -127,9 +118,9 @@
         return table.at[pl.ds(pl.multiple_of(start, 16), share)]
 
     def leg_copy(k, i):
-        rows = rows_of(me_l, me_f, me_e, i)
+        start = pl.multiple_of((me_e * chunks + i) * share, 16)
         return pltpu.make_async_remote_copy(
-            src_ref=rows, dst_ref=rows,
+            src_ref=leg_ref.at[pl.ds(start, share)], dst_ref=rows_of(me_l, me_f, me_e, i),
             send_sem=leg_send.at[k, i], recv_sem=leg_recv.at[k, i],
             device_id={"lev": lax.rem(me_l + k, lev)}, device_id_type=MESH,
         )
@@ -153,7 +144,7 @@
         )
 
     own_copy = pltpu.make_async_remote_copy(
-        src_ref=quarter(me_l, me_f), dst_ref=quarter(me_l, me_f),
+        src_ref=leg_ref, dst_ref=quarter(me_l, me_f),
         send_sem=own_send.at[0], recv_sem=own_recv.at[0],
         device_id={"fld": 1 - me_f}, device_id_type=MESH,
     )
@@ -176,7 +167,6 @@
     fwd_copies = [
         [[fwd_copy(k, q, i) for i in range(chunks)] for q in range(ens)] for k in range(1, lev)
     ]
-    table_copy.wait()
     for row in leg_copies:
         for copy in row:
             copy.start()
@@ -192,8 +182,6 @@
             there = lax.rem(me_w + k, wide)
             pair_rows(f, there, x_ref, there)
 
-    for copy in level_copies:
-        copy.wait()
     rates[...] = expand_rates(rate_ref, lev * columns)
     whole_into = expand(to_ref, lev * columns)
     whole_back = expand(from_ref, lev * columns)
@@ -217,6 +205,7 @@
     for f in range(1, fields):
         for copy in in_copies[f]:
             copy.start()
+    table_copy.wait()
     own_copy.wait_recv()
     for k in range(lev - 1):
         for q in range(ens):
@@ -424,13 +413,9 @@
             jax.ShapeDtypeStruct((2, rows, columns), jnp.bfloat16),
             jax.ShapeDtypeStruct((degrees * fields, columns), jnp.bfloat16),
         ),
-        in_specs=[smem] + [pl.BlockSpec(memory_space=pltpu.HBM)] * 6,
+        in_specs=[smem, vmem, pl.BlockSpec(memory_space=pl.ANY), vmem, vmem, vmem, vmem],
         out_specs=(vmem, vmem),
         scratch_shapes=[
-            pltpu.VMEM((2, rows, columns), jnp.bfloat16),
-            pltpu.VMEM(to_modes.shape, jnp.bfloat16),
-            pltpu.VMEM(from_modes.shape, jnp.bfloat16),
-            pltpu.VMEM((1, mode_rate.shape[0]), jnp.float32),
             pltpu.VMEM((own_rows, columns), jnp.float32),
             pltpu.VMEM((2, rows, columns), jnp.float32),
             pltpu.VMEM(blocks, held),
@@ -452,7 +437,7 @@
             dma((fields, wide)),
             dma((lev, chunks)),
             dma((lev, chunks)),
-            dma((7,)),
+            dma((2,)),
             dma((lev, ens, chunks)),
             dma((lev, ens, chunks)),
             dma((1,)),
@@ -467,7 +452,7 @@
             dma((fields, wide)),
         ],
         compiler_params=pltpu.CompilerParams(
-            collective_id=0, has_side_effects=True, vmem_limit_bytes=36 * 2**20
+            collective_id=0, has_side_effects=True, vmem_limit_bytes=56 * 2**20
         ),
     )(
         slot_wave, given, latitude_weights(latitudes, columns), legendre[0],

time: 71.9 us -> 71 us (0.987)
  local copies, waits for them, and re-layouts: 7.6 us -> 4.18 us
  Pallas kernels: 61.6 us -> 64.4 us
    unnamed x14 -> x4, local copies, waits for them, and re-layouts: 7.6 us -> 4.18 us
    pallas_call x1, Pallas kernels: 61.6 us -> 64.4 us  [shards(): pl.pallas_call(functools.partial(step, (ens, wide, lev, chunks)), out_sha...]
where the time goes in v4:
time: 71 us; the launch traced here: 69.8 us
  Pallas kernels  64.4 us (91%)
  local copies, waits for them, and re-layouts  4.18 us (6%)
  between operations  1.29 us (2%)
    pallas_call x1, Pallas kernels, shards(): pl.pallas_call(functools.partial(step, (ens, wide, lev, chunks)), out_sha...  64.4 us
    unnamed x4, local copies, waits for them, and re-layouts  4.18 us

profile of v4, /device:TPU:0, one launch (start us, length us, event | category | flops | bytes accessed | tf_op | source)
XLA Modules:
  0.0 69.8 jit_solution(9982313591119895321)
XLA Ops:
  1.3 64.4 %shard_map.86 = (bf16[2,2560,128]{2,1,0:T(8,128)(2,1)}, bf16[2560,128]{1,0:T(8,128)(2,1)}) custom-call(s32[1]{0:T(128)S(6)} %copy.11.wave_ref, bf16[2,2560,128]{2,1,0:T(8,128)(2,1)} %bitcast.5, f32[1280,128]{1,0:T(8,128)} %constant.2.clone.weight_ref, bf16[320,1280]{1,0:T(8,128)(2,1)} %bitcast.7, bf16[128,128]{1,0:T(8,128)(2,1)} %to_ref.1, ...), custom_call_target="tpu_custom_call" | custom-call | tf_op jit(solution)/shard_map/pallas_call | solution.py:410
  65.7 0.0 copy-start
  65.7 3.3 %copy.12 = bf16[2,320,4,2,128]{4,3,2,1,0:T(2,128)(2,1)} copy(bf16[2,320,4,2,128]{4,3,2,1,0:T(2,128)(2,1)} %bitcast.6) | data formatting | bytes 2621440
  69.0 0.0 copy-done
  69.0 0.8 %copy.13 = bf16[1,1280,2,128]{3,2,1,0:T(2,128)(2,1)} copy(bf16[1,1280,2,128]{3,2,1,0:T(2,128)(2,1)S(1)} %bitcast.8) | data formatting | bytes 1310720
Async XLA Ops:
  65.7 3.3 %copy-start = (bf16[2560,128]{1,0:T(8,128)(2,1)S(1)}, bf16[2560,128]{1,0:T(8,128)(2,1)}, u32[]{:S(2)}) copy-start(bf16[2560,128]{1,0:T(8,128)(2,1)} %get-tuple-element.5) | copy-start | bytes 1966084
